TPU v7x, 32 devices: a whole 2x2x4 slice. The times are simulated.
32 devices in a mesh: sc: 4 (over y, x), rows: 8 (over z, core).
Axes of the slice: x: 2, y: 2, z: 4, core: 2. Of those that a mesh axis runs over, the one named last changes fastest.
Arguments:
- embeddings: bfloat16 [32768, 1024], P(('sc', 'rows')), may hold values from -6 to 6
- labels: int32 [32768, 1], P(('sc', 'rows')), may hold values from 0 to 3; in each aligned block of 1024 rows (0 to 1023, 1024 to 2047, ...) at most 512 rows name the same one
- init_idx: int32 [4, 256], P('sc'), may hold values from 0 to 16383
Outputs:
- assign: bfloat16 [32768, 256], P(('sc', 'rows'))
- centroids: float32 [4, 256, 1024], P('sc')
Inputs may be any that keep to these rules, and one draw needn't show every extreme that they name: `labels`: among the rows of one device (aligned blocks of 1024 rows) no label occurs more than 512 times, and some label occurs exactly 512 times; every label occurs somewhere.
All inputs are finite; a program needn't handle non-finite values.
Results may differ from a plain program's by a relative error of at most 0.0052.
Values may be sent and summed in bfloat16 or wider, within the bound.
A program may use at most 64 MiB of HBM per device.

v0:
```python
import math
import jax
import jax.numpy as jnp
from jax import lax
from jax.sharding import PartitionSpec as P

ITERS = 3
ROUNDS = 3


def carried_in(part, axis, combine, identity):
    place = lax.axis_index(axis)
    gathered = lax.all_gather(part, axis)
    state = jnp.zeros_like(part) + jnp.asarray(identity, part.dtype)

    def one(turn, state):
        return combine(state, lax.dynamic_index_in_dim(gathered, turn, 0, False))

    return lax.fori_loop(0, place, one, state)


def unit_of(rows):
    values = rows.astype(jnp.float32)
    scale = lax.rsqrt(jnp.mean(values * values, axis=1, keepdims=True) + 1e-05) * (
        1.0 / math.sqrt(rows.shape[1])
    )
    return (values * scale).astype(jnp.bfloat16)


def unit_cent(mass):
    return (mass * lax.rsqrt(jnp.sum(mass * mass, axis=1, keepdims=True) + 1e-06)).astype(
        jnp.bfloat16
    )


def on_device(embeddings, labels, init_idx):
    tok = embeddings.shape[0]
    width = embeddings.shape[1]
    groups = lax.axis_size("sc")
    slots = 2 * tok // groups
    label_col = labels[:, 0]
    member = (label_col[:, None] == jnp.arange(groups, dtype=jnp.int32)[None, :]).astype(jnp.int32)
    before_here = jnp.cumsum(member, axis=0) - member
    place = jnp.sum(before_here * member, axis=1)
    counts = jnp.sum(member, axis=0).astype(jnp.float32)
    prefix = carried_in(
        counts, ("sc", "rows"), lambda early, later: early + later, jnp.zeros_like(counts)
    )
    totals = lax.psum(counts, ("sc", "rows"))
    prefix_int = prefix.astype(jnp.int32)
    totals_int = totals.astype(jnp.int32)
    rank = jnp.sum(member * prefix_int[None, :], axis=1) + place
    target = label_col * slots + place
    source = (
        jnp.full((groups * slots,), tok, jnp.int32).at[target].set(jnp.arange(tok, dtype=jnp.int32))
    )
    padded = jnp.concatenate([embeddings, jnp.zeros((1, width), jnp.bfloat16)], axis=0)
    rank_pad = jnp.concatenate([rank, jnp.full((1,), -1, jnp.int32)], axis=0)
    outgoing = padded[source].reshape(groups, slots, width)
    out_rank = rank_pad[source].reshape(groups, slots)
    incoming, in_rank = (
        lax.all_to_all(outgoing, "sc", split_axis=0, concat_axis=0, tiled=True),
        lax.all_to_all(out_rank, "sc", split_axis=0, concat_axis=0, tiled=True),
    )
    incoming = incoming.reshape(groups * slots, width)
    in_rank = in_rank.reshape(groups * slots)
    valid = in_rank >= 0
    members = unit_of(incoming)
    group_here = lax.axis_index("sc")
    count = jnp.sum(jnp.where(jnp.arange(groups, dtype=jnp.int32) == group_here, totals_int, 0))
    wanted = init_idx[0] % count
    picker = (wanted[:, None] == in_rank[None, :]).astype(jnp.bfloat16)
    seeds = jnp.dot(picker, members, preferred_element_type=jnp.float32)
    cent = lax.psum(seeds, "rows").astype(jnp.bfloat16)
    contract_rows = (((0,), (0,)), ((), ()))
    contract_width = (((1,), (1,)), ((), ()))
    for round_index in range(ROUNDS):
        scores = lax.dot_general(members, cent, contract_width, preferred_element_type=jnp.float32)
        plan = jnp.where(valid[:, None], jnp.exp(scores * 10.0), 0.0)
        for step in range(ITERS):
            column = lax.psum(jnp.sum(plan, axis=0), "rows")
            plan = plan / column[None, :]
            row_sum = jnp.sum(plan, axis=1)
            plan = jnp.where(valid[:, None], plan / jnp.where(valid, row_sum, 1.0)[:, None], 0.0)
        plan_b = plan.astype(jnp.bfloat16)
        mass_part = lax.dot_general(
            plan_b, members, contract_rows, preferred_element_type=jnp.float32
        )
        if round_index < ROUNDS - 1:
            mass = lax.psum(mass_part, "rows")
            cent = unit_cent(mass)
        else:
            weight_part = jnp.sum(plan, axis=0)
            mass, weight = lax.psum((mass_part, weight_part), "rows")
            means = mass / weight[:, None]
    plan_out = plan.astype(jnp.bfloat16).reshape(groups, slots, plan.shape[1])
    returned = lax.all_to_all(plan_out, "sc", split_axis=0, concat_axis=0, tiled=True).reshape(
        groups * slots, plan.shape[1]
    )
    assign = returned[target]
    return (assign, means[None])


def solution(mesh):
    return jax.shard_map(
        on_device,
        mesh=mesh,
        in_specs=(P(("sc", "rows"), None), P(("sc", "rows"), None), P("sc", None)),
        out_specs=(P(("sc", "rows"), None), P("sc", None, None)),
        check_vma=False,
    )
```

profile of v0, /device:TPU:0, one launch (start us, length us, event | category | flops | bytes accessed | tf_op | source)
XLA Modules:
  0.0 568.7 jit_solution(1118507430221130394)
XLA Ops:
  8.1 42.0 %all-reduce.2 = (f32[128]{0:T(128)S(1)}, f32[4]{0:T(128)S(1)}) all-reduce(f32[128]{0:T(128)S(1)} %convert_dynamic-update-slice_fusion, f32[4]{0:T(128)S(1)} %convert_element_type.59), channel_id=2, replica_groups=mesh['sc'=4,'rows'=8] {'sc','rows'}, use_global_device_ids=true, to_apply=%add.1 | all-reduce | flops 132 | bytes 1056
  54.0 4.3 scatter_custom_fusion
  58.4 20.6 %gather_fusion = s32[2048]{0:T(1024)} fusion(s32[1025]{0:T(1024)S(1)} %pad_add_fusion, s32[2048]{0:T(1024)S(1)} %fusion.27), kind=kCustom, calls=%fused_computation | custom fusion | bytes 24576 | tf_op jit(solution)/shard_map/gather | solution.py:60
  78.9 4.4 all-to-all-start
  85.1 9.7 %gather_fusion.1 = bf16[2048,1024]{1,0:T(8,128)(2,1)} fusion(bf16[1025,1024]{1,0:T(8,128)(2,1)S(1)} %concatenate.7, s32[2048]{0:T(1024)S(1)} %fusion.27), kind=kCustom, calls=%fused_computation.1 | custom fusion | bytes 8396800 | tf_op jit(solution)/shard_map/gather | solution.py:59
  94.8 5.0 all-to-all-start.1
  101.9 44.5 %all-to-all-done.1 = bf16[4,512,1024]{2,1,0:T(8,128)(2,1)} async-done(((bf16[4,512,1024]{2,1,0:T(8,128)(2,1)}), bf16[4,512,1024]{2,1,0:T(8,128)(2,1)}, u32[]{:S(2)}, u32[]{:S(2)}) %all-to-all-start.1) | async-done | bytes 4194336 | tf_op jit(solution)/shard_map/all_to_all | solution.py:62
  146.5 3.1 multiply_reduce_fusion
  149.6 2.9 fusion
  155.8 57.9 %all-reduce.13 = bf16[256,1024]{1,0:T(8,128)(2,1)S(1)} all-reduce(f32[256,1024]{1,0:T(8,128)S(1)} %fusion.7), channel_id=1, replica_groups=mesh['sc'=4,'rows'=8] {'rows'}, use_global_device_ids=true, to_apply=%region_11.12 | all-reduce | flops 262144 | bytes 1572864 | tf_op jit(solution)/shard_map/psum | solution.py:74
  213.7 3.2 fusion.41
  216.8 15.1 %psum.107 = f32[256]{0:T(256)S(1)} all-reduce(f32[256]{0:T(256)S(1)} %get-tuple-element.52), channel_id=1, replica_groups=mesh['sc'=4,'rows'=8] {'rows'}, use_global_device_ids=true, to_apply=%region_13.14 | all-reduce | flops 256 | bytes 2048 | tf_op jit(solution)/shard_map/psum | solution.py:81
  234.3 13.6 %psum.108 = f32[256]{0:T(256)S(1)} all-reduce(f32[256]{0:T(256)S(1)} %get-tuple-element.48), channel_id=1, replica_groups=mesh['sc'=4,'rows'=8] {'rows'}, use_global_device_ids=true, to_apply=%region_16.17 | all-reduce | flops 256 | bytes 2048 | tf_op jit(solution)/shard_map/psum | solution.py:81
  250.0 13.7 %psum.109 = f32[256]{0:T(256)S(1)} all-reduce(f32[256]{0:T(256)S(1)} %get-tuple-element.46), channel_id=1, replica_groups=mesh['sc'=4,'rows'=8] {'rows'}, use_global_device_ids=true, to_apply=%region_19.20 | all-reduce | flops 256 | bytes 2048 | tf_op jit(solution)/shard_map/psum | solution.py:81
  265.7 4.9 fusion.9
  270.9 56.0 %all-reduce.8.cloned.1.call-done = f32[256,1024]{1,0:T(8,128)} async-done(((f32[256,1024]{1,0:T(8,128)}), f32[256,1024]{1,0:T(8,128)}) %all-reduce.8.cloned.1.call-update) | async-done | bytes 1048592 | tf_op jit(solution)/shard_map/psum | solution.py:90
  328.2 3.6 fusion.42
  331.8 13.6 %psum.111 = f32[256]{0:T(256)S(1)} all-reduce(f32[256]{0:T(256)S(1)} %get-tuple-element.54), channel_id=1, replica_groups=mesh['sc'=4,'rows'=8] {'rows'}, use_global_device_ids=true, to_apply=%region_24.25 | all-reduce | flops 256 | bytes 2048 | tf_op jit(solution)/shard_map/psum | solution.py:81
  347.7 13.6 %psum.112 = f32[256]{0:T(256)S(1)} all-reduce(f32[256]{0:T(256)S(1)} %get-tuple-element.44), channel_id=1, replica_groups=mesh['sc'=4,'rows'=8] {'rows'}, use_global_device_ids=true, to_apply=%region_27.28 | all-reduce | flops 256 | bytes 2048 | tf_op jit(solution)/shard_map/psum | solution.py:81
  363.4 13.7 %psum.113 = f32[256]{0:T(256)S(1)} all-reduce(f32[256]{0:T(256)S(1)} %get-tuple-element.42), channel_id=1, replica_groups=mesh['sc'=4,'rows'=8] {'rows'}, use_global_device_ids=true, to_apply=%region_30.31 | all-reduce | flops 256 | bytes 2048 | tf_op jit(solution)/shard_map/psum | solution.py:81
  379.1 4.9 fusion.10
  384.1 57.0 %all-reduce.10.cloned.1.call-done = f32[256,1024]{1,0:T(8,128)} async-done(((f32[256,1024]{1,0:T(8,128)}), f32[256,1024]{1,0:T(8,128)}) %all-reduce.10.cloned.1.call-update) | async-done | bytes 1048592 | tf_op jit(solution)/shard_map/psum | solution.py:90
  442.5 3.6 fusion.43
  446.1 13.6 %psum.115 = f32[256]{0:T(256)S(1)} all-reduce(f32[256]{0:T(256)S(1)} %get-tuple-element.56), channel_id=1, replica_groups=mesh['sc'=4,'rows'=8] {'rows'}, use_global_device_ids=true, to_apply=%region_35.36 | all-reduce | flops 256 | bytes 2048 | tf_op jit(solution)/shard_map/psum | solution.py:81
  462.1 13.6 %psum.116 = f32[256]{0:T(256)S(1)} all-reduce(f32[256]{0:T(256)S(1)} %get-tuple-element.40), channel_id=1, replica_groups=mesh['sc'=4,'rows'=8] {'rows'}, use_global_device_ids=true, to_apply=%region_38.39 | all-reduce | flops 256 | bytes 2048 | tf_op jit(solution)/shard_map/psum | solution.py:81
  478.0 13.6 %psum.117 = f32[256]{0:T(256)S(1)} all-reduce(f32[256]{0:T(256)S(1)} %get-tuple-element.38), channel_id=1, replica_groups=mesh['sc'=4,'rows'=8] {'rows'}, use_global_device_ids=true, to_apply=%region_41.42 | all-reduce | flops 256 | bytes 2048 | tf_op jit(solution)/shard_map/psum | solution.py:81
  494.2 3.5 fusion.44
  497.7 3.6 all-to-all-start.2
  501.3 13.9 %psum.119 = f32[256]{0:T(256)S(1)} all-reduce(f32[256]{0:T(256)S(1)} %get-tuple-element.50), channel_id=1, replica_groups=mesh['sc'=4,'rows'=8] {'rows'}, use_global_device_ids=true, to_apply=%region_45.46 | all-reduce | flops 256 | bytes 2048 | tf_op jit(solution)/shard_map/psum | solution.py:94
  515.2 39.6 %all-reduce.12.cloned.1.call-done = f32[256,1024]{1,0:T(8,128)} async-done(((f32[256,1024]{1,0:T(8,128)}), f32[256,1024]{1,0:T(8,128)}) %all-reduce.12.cloned.1.call-update) | async-done | bytes 1048592 | tf_op jit(solution)/shard_map/psum | solution.py:94
  554.8 2.3 divide_bitcast_fusion
  557.2 5.0 gather_fusion.2
  (83 shorter events, 33.6 us)
Async XLA Ops:
  78.9 15.9 %all-to-all-start = ((s32[4,1,512]{2,1,0:T(1,128)}), s32[4,1,512]{2,1,0:T(1,128)S(1)}, u32[]{:S(2)}, u32[]{:S(2)}) async-start(s32[4,1,512]{2,1,0:T(1,128)} %bitcast.6), calls=%async_computation | async-start | bytes 16384 | tf_op jit(solution)/shard_map/all_to_all | solution.py:63
  94.8 7.0 %copy-start.8 = (s32[1,256]{1,0:T(1,128)S(1)}, s32[1,256]{1,0:T(1,128)}, u32[]{:S(2)}) copy-start(s32[1,256]{1,0:T(1,128)} %param.7) | copy-start | bytes 3076
  94.8 51.7 %all-to-all-start.1 = ((bf16[4,512,1024]{2,1,0:T(8,128)(2,1)}), bf16[4,512,1024]{2,1,0:T(8,128)(2,1)}, u32[]{:S(2)}, u32[]{:S(2)}) async-start(bf16[4,512,1024]{2,1,0:T(8,128)(2,1)} %bitcast.45), calls=%async_computation.1 | async-start | bytes 8388608 | tf_op jit(solution)/shard_map/all_to_all | solution.py:62
  99.8 227.1 %all-reduce.8.cloned.1.call-start = ((), (), s32[]{:S(2)}) async-start(), calls=%async_computation.3 | async-start | bytes 2097152 | tf_op jit(solution)/shard_map/psum | solution.py:90
  152.5 1.9 copy-start.6
  216.8 15.5 %copy-start.3 = (f32[2048,256]{1,0:T(8,128)}, f32[2048,256]{1,0:T(8,128)S(1)}, u32[]{:S(2)}) copy-start(f32[2048,256]{1,0:T(8,128)S(1)} %get-tuple-element.53) | copy-start | bytes 6291460
  250.0 15.7 %copy-start.4 = (f32[2048,256]{1,0:T(8,128)S(1)}, f32[2048,256]{1,0:T(8,128)}, u32[]{:S(2)}) copy-start(f32[2048,256]{1,0:T(8,128)} %get-tuple-element.47) | copy-start | bytes 6291460
  270.6 170.5 %all-reduce.10.cloned.1.call-start = ((), (), s32[]{:S(2)}) async-start(), calls=%async_computation.4 | async-start | bytes 2097152 | tf_op jit(solution)/shard_map/psum | solution.py:90
  331.8 14.0 %copy-start.1 = (f32[2048,256]{1,0:T(8,128)}, f32[2048,256]{1,0:T(8,128)S(1)}, u32[]{:S(2)}) copy-start(f32[2048,256]{1,0:T(8,128)S(1)} %get-tuple-element.55) | copy-start | bytes 6291460
  363.4 15.7 %copy-start.5 = (f32[2048,256]{1,0:T(8,128)S(1)}, f32[2048,256]{1,0:T(8,128)}, u32[]{:S(2)}) copy-start(f32[2048,256]{1,0:T(8,128)} %get-tuple-element.43) | copy-start | bytes 6291460
  384.1 170.8 %all-reduce.12.cloned.1.call-start = ((), (), s32[]{:S(2)}) async-start(), calls=%async_computation.5 | async-start | bytes 2097152 | tf_op jit(solution)/shard_map/psum | solution.py:94
  446.1 14.0 %copy-start.2 = (f32[2048,256]{1,0:T(8,128)}, f32[2048,256]{1,0:T(8,128)S(1)}, u32[]{:S(2)}) copy-start(f32[2048,256]{1,0:T(8,128)S(1)} %get-tuple-element.57) | copy-start | bytes 6291460
  462.1 14.0 %copy-start = (f32[2048,256]{1,0:T(8,128)}, f32[2048,256]{1,0:T(8,128)S(1)}, u32[]{:S(2)}) copy-start(f32[2048,256]{1,0:T(8,128)S(1)} %get-tuple-element.41) | copy-start | bytes 6291460
  491.6 2.6 copy-start.7
  497.7 59.5 %all-to-all-start.2 = ((bf16[4,512,256]{2,1,0:T(8,128)(2,1)}), bf16[4,512,256]{2,1,0:T(8,128)(2,1)S(1)}, u32[]{:S(2)}, u32[]{:S(2)}) async-start(bf16[4,512,256]{2,1,0:T(8,128)(2,1)} %bitcast.11), calls=%async_computation.2 | async-start | bytes 2097152 | tf_op jit(solution)/shard_map/all_to_all | solution.py:97
Sparse Core Ops, SparseCore 0:
  270.8 56.0 all-reduce.7
  384.2 56.9 all-reduce.9
  497.8 56.9 all-reduce.11
where the time goes:
time: 570 us; the launch traced here: 569 us
  blocking collectives  238 us (42%)
  waiting for transfers between devices  197 us (35%)
  local copies, waits for them, and re-layouts  44.2 us (8%)
  other arithmetic  35.6 us (6%)
  matrix products  25 us (4%)
  between operations  15.5 us (3%)
  starting transfers between devices  13.4 us (2%)
    psum x9, blocking collectives, on_device(): column = lax.psum(jnp.sum(plan, axis=0), 'rows')  124 us
    psum x2, waiting for transfers between devices, on_device(): mass = lax.psum(mass_part, 'rows')  113 us
    psum x1, blocking collectives, on_device(): cent = lax.psum(seeds, 'rows').astype(jnp.bfloat16)  57.9 us
    all_to_all x1, waiting for transfers between devices, on_device(): lax.all_to_all(outgoing, 'sc', split_axis=0, concat_axis=0, tiled=True)  44.5 us
    unnamed x1, blocking collectives  42 us
    psum x1, waiting for transfers between devices, on_device(): mass, weight = lax.psum((mass_part, weight_part), 'rows')  39.6 us
    gather x1, local copies, waits for them, and re-layouts, on_device(): out_rank = rank_pad[source].reshape(groups, slots)  20.6 us
    psum x1, blocking collectives, on_device(): mass, weight = lax.psum((mass_part, weight_part), 'rows')  13.9 us
  transfers between devices with their start and end apart: 6, of which 4 were waited for; matrix products, arithmetic and copies ran while one was open for 3% of the time, Pallas kernels for 0%

commit v1 on v0

--- a/solution.py
+++ b/solution.py
@@ -6,6 +6,22 @@
 
 ITERS = 3
 ROUNDS = 3
+
+
+def exchange_in_pairs(array, axis, split, join):
+    ways, here = (lax.axis_size(axis), lax.axis_index(axis))
+    width = array.shape[split] // ways
+    lengths = list(array.shape)
+    lengths[split] = width
+    height = lengths[join]
+    lengths[join] = height * ways
+    full = jnp.zeros(lengths, array.dtype)
+    for mask in range(ways):
+        part = lax.dynamic_slice_in_dim(array, (here ^ mask) * width, width, axis=split)
+        if mask:
+            part = lax.ppermute(part, axis, [(d, d ^ mask) for d in range(ways)])
+        full = lax.dynamic_update_slice_in_dim(full, part, (here ^ mask) * height, axis=join)
+    return full
 
 
 def carried_in(part, axis, combine, identity):
@@ -59,7 +75,7 @@
     outgoing = padded[source].reshape(groups, slots, width)
     out_rank = rank_pad[source].reshape(groups, slots)
     incoming, in_rank = (
-        lax.all_to_all(outgoing, "sc", split_axis=0, concat_axis=0, tiled=True),
+        exchange_in_pairs(outgoing, "sc", 0, 0),
         lax.all_to_all(out_rank, "sc", split_axis=0, concat_axis=0, tiled=True),
     )
     incoming = incoming.reshape(groups * slots, width)

time: 570 us -> 550 us (0.965)
  waiting for transfers between devices: 197 us -> 169 us
  local copies, waits for them, and re-layouts: 44.2 us -> 53.9 us
    all_to_all x1 -> x0, waiting for transfers between devices: 44.5 us -> none  [on_device(): lax.all_to_all(outgoing, 'sc', split_axis=0, concat_axis=0, tiled=True)]
    ppermute x0 -> x3, waiting for transfers between devices: none -> 15.2 us  [exchange_in_pairs(): part = lax.ppermute(part, axis, [(d, d ^ mask) for d in range(ways)])]
    dynamic_update_slice x0 -> x3, local copies, waits for them, and re-layouts: none -> 6.88 us  [exchange_in_pairs(): lax.dynamic_update_slice_in_dim(full, part, (here ^ mask) * height, axis=...]
    ppermute x0 -> x3, starting transfers between devices: none -> 6.63 us  [exchange_in_pairs(): part = lax.ppermute(part, axis, [(d, d ^ mask) for d in range(ways)])]
  transfers between devices with their start and end apart: 6 -> 8, of which waited for: 4 -> 4; matrix products, arithmetic and copies ran while one was open for 3% -> 5% of each run, Pallas kernels for 0% -> 0%
where the time goes in v1:
time: 550 us; the launch traced here: 549 us
  blocking collectives  238 us (43%)
  waiting for transfers between devices  169 us (31%)
  local copies, waits for them, and re-layouts  53.9 us (10%)
  other arithmetic  33.5 us (6%)
  matrix products  25 us (5%)
  between operations  15.6 us (3%)
  starting transfers between devices  13.6 us (2%)
    psum x9, blocking collectives, on_device(): column = lax.psum(jnp.sum(plan, axis=0), 'rows')  126 us
    psum x2, waiting for transfers between devices, on_device(): mass = lax.psum(mass_part, 'rows')  114 us
    psum x1, blocking collectives, on_device(): cent = lax.psum(seeds, 'rows').astype(jnp.bfloat16)  56.3 us
    unnamed x1, blocking collectives  42 us
    psum x1, waiting for transfers between devices, on_device(): mass, weight = lax.psum((mass_part, weight_part), 'rows')  39.6 us
    gather x1, local copies, waits for them, and re-layouts, on_device(): out_rank = rank_pad[source].reshape(groups, slots)  20.6 us
    ppermute x3, waiting for transfers between devices, exchange_in_pairs(): part = lax.ppermute(part, axis, [(d, d ^ mask) for d in range(ways)])  15.2 us
    psum x1, blocking collectives, on_device(): mass, weight = lax.psum((mass_part, weight_part), 'rows')  13.9 us
  transfers between devices with their start and end apart: 8, of which 4 were waited for; matrix products, arithmetic and copies ran while one was open for 5% of the time, Pallas kernels for 0%

profile of v1, /device:TPU:0, one launch (start us, length us, event | category | flops | bytes accessed | tf_op | source)
XLA Modules:
  0.0 548.9 jit_solution(11140179678903276871)
XLA Ops:
  8.1 42.0 %all-reduce.2 = (f32[128]{0:T(128)S(1)}, f32[4]{0:T(128)S(1)}) all-reduce(f32[128]{0:T(128)S(1)} %convert_dynamic-update-slice_fusion, f32[4]{0:T(128)S(1)} %convert_element_type.59), channel_id=2, replica_groups=mesh['sc'=4,'rows'=8] {'sc','rows'}, use_global_device_ids=true, to_apply=%add.1 | all-reduce | flops 132 | bytes 1056
  54.0 4.3 scatter_custom_fusion
  60.1 9.7 %gather_fusion.1 = bf16[2048,1024]{1,0:T(8,128)(2,1)} fusion(bf16[1025,1024]{1,0:T(8,128)(2,1)S(1)} %concatenate.7, s32[2048]{0:T(1024)S(1)} %fusion.27), kind=kCustom, calls=%fused_computation.1 | custom fusion | bytes 8396800 | tf_op jit(solution)/shard_map/gather | solution.py:75
  72.4 2.6 collective-permute-start
  76.3 20.6 %gather_fusion = s32[2048]{0:T(1024)} fusion(s32[1025]{0:T(1024)S(1)} %pad_add_fusion, s32[2048]{0:T(1024)S(1)} %fusion.27), kind=kCustom, calls=%fused_computation | custom fusion | bytes 24576 | tf_op jit(solution)/shard_map/gather | solution.py:76
  96.8 3.2 all-to-all-start
  100.1 2.8 collective-permute-start.2
  109.7 15.2 %collective-permute-done.2 = bf16[1,512,1024]{2,1,0:T(8,128)(2,1)} collective-permute-done((bf16[1,512,1024]{2,1,0:T(8,128)(2,1)S(1)}, bf16[1,512,1024]{2,1,0:T(8,128)(2,1)}, u32[]{:S(2)}, u32[]{:S(2)}) %collective-permute-start.2) | collective-permute-done | bytes 1048608 | tf_op jit(solution)/shard_map/ppermute | solution.py:22
  127.2 3.2 multiply_reduce_fusion
  134.7 56.3 %all-reduce.13 = bf16[256,1024]{1,0:T(8,128)(2,1)S(1)} all-reduce(f32[256,1024]{1,0:T(8,128)S(1)} %fusion.7), channel_id=1, replica_groups=mesh['sc'=4,'rows'=8] {'rows'}, use_global_device_ids=true, to_apply=%region_11.12 | all-reduce | flops 262144 | bytes 1572864 | tf_op jit(solution)/shard_map/psum | solution.py:90
  191.0 3.2 fusion.41
  194.2 16.7 %psum.107 = f32[256]{0:T(256)S(1)} all-reduce(f32[256]{0:T(256)S(1)} %get-tuple-element.56), channel_id=1, replica_groups=mesh['sc'=4,'rows'=8] {'rows'}, use_global_device_ids=true, to_apply=%region_13.14 | all-reduce | flops 256 | bytes 2048 | tf_op jit(solution)/shard_map/psum | solution.py:97
  213.2 13.6 %psum.108 = f32[256]{0:T(256)S(1)} all-reduce(f32[256]{0:T(256)S(1)} %get-tuple-element.48), channel_id=1, replica_groups=mesh['sc'=4,'rows'=8] {'rows'}, use_global_device_ids=true, to_apply=%region_16.17 | all-reduce | flops 256 | bytes 2048 | tf_op jit(solution)/shard_map/psum | solution.py:97
  228.9 13.9 %psum.109 = f32[256]{0:T(256)S(1)} all-reduce(f32[256]{0:T(256)S(1)} %get-tuple-element.46), channel_id=1, replica_groups=mesh['sc'=4,'rows'=8] {'rows'}, use_global_device_ids=true, to_apply=%region_19.20 | all-reduce | flops 256 | bytes 2048 | tf_op jit(solution)/shard_map/psum | solution.py:97
  244.8 4.9 fusion.9
  249.8 57.2 %all-reduce.8.cloned.1.call-done = f32[256,1024]{1,0:T(8,128)} async-done(((f32[256,1024]{1,0:T(8,128)}), f32[256,1024]{1,0:T(8,128)}) %all-reduce.8.cloned.1.call-update) | async-done | bytes 1048592 | tf_op jit(solution)/shard_map/psum | solution.py:106
  308.3 3.6 fusion.42
  311.9 13.6 %psum.111 = f32[256]{0:T(256)S(1)} all-reduce(f32[256]{0:T(256)S(1)} %get-tuple-element.58), channel_id=1, replica_groups=mesh['sc'=4,'rows'=8] {'rows'}, use_global_device_ids=true, to_apply=%region_24.25 | all-reduce | flops 256 | bytes 2048 | tf_op jit(solution)/shard_map/psum | solution.py:97
  327.9 13.6 %psum.112 = f32[256]{0:T(256)S(1)} all-reduce(f32[256]{0:T(256)S(1)} %get-tuple-element.44), channel_id=1, replica_groups=mesh['sc'=4,'rows'=8] {'rows'}, use_global_device_ids=true, to_apply=%region_27.28 | all-reduce | flops 256 | bytes 2048 | tf_op jit(solution)/shard_map/psum | solution.py:97
  343.6 13.7 %psum.113 = f32[256]{0:T(256)S(1)} all-reduce(f32[256]{0:T(256)S(1)} %get-tuple-element.42), channel_id=1, replica_groups=mesh['sc'=4,'rows'=8] {'rows'}, use_global_device_ids=true, to_apply=%region_30.31 | all-reduce | flops 256 | bytes 2048 | tf_op jit(solution)/shard_map/psum | solution.py:97
  359.2 4.9 fusion.10
  364.2 57.1 %all-reduce.10.cloned.1.call-done = f32[256,1024]{1,0:T(8,128)} async-done(((f32[256,1024]{1,0:T(8,128)}), f32[256,1024]{1,0:T(8,128)}) %all-reduce.10.cloned.1.call-update) | async-done | bytes 1048592 | tf_op jit(solution)/shard_map/psum | solution.py:106
  422.7 3.6 fusion.43
  426.3 13.6 %psum.115 = f32[256]{0:T(256)S(1)} all-reduce(f32[256]{0:T(256)S(1)} %get-tuple-element.60), channel_id=1, replica_groups=mesh['sc'=4,'rows'=8] {'rows'}, use_global_device_ids=true, to_apply=%region_35.36 | all-reduce | flops 256 | bytes 2048 | tf_op jit(solution)/shard_map/psum | solution.py:97
  442.3 13.6 %psum.116 = f32[256]{0:T(256)S(1)} all-reduce(f32[256]{0:T(256)S(1)} %get-tuple-element.40), channel_id=1, replica_groups=mesh['sc'=4,'rows'=8] {'rows'}, use_global_device_ids=true, to_apply=%region_38.39 | all-reduce | flops 256 | bytes 2048 | tf_op jit(solution)/shard_map/psum | solution.py:97
  458.2 13.6 %psum.117 = f32[256]{0:T(256)S(1)} all-reduce(f32[256]{0:T(256)S(1)} %get-tuple-element.38), channel_id=1, replica_groups=mesh['sc'=4,'rows'=8] {'rows'}, use_global_device_ids=true, to_apply=%region_41.42 | all-reduce | flops 256 | bytes 2048 | tf_op jit(solution)/shard_map/psum | solution.py:97
  474.4 3.5 fusion.44
  477.9 3.6 all-to-all-start.1
  481.5 13.9 %psum.119 = f32[256]{0:T(256)S(1)} all-reduce(f32[256]{0:T(256)S(1)} %get-tuple-element.54), channel_id=1, replica_groups=mesh['sc'=4,'rows'=8] {'rows'}, use_global_device_ids=true, to_apply=%region_45.46 | all-reduce | flops 256 | bytes 2048 | tf_op jit(solution)/shard_map/psum | solution.py:110
  495.4 39.6 %all-reduce.12.cloned.1.call-done = f32[256,1024]{1,0:T(8,128)} async-done(((f32[256,1024]{1,0:T(8,128)}), f32[256,1024]{1,0:T(8,128)}) %all-reduce.12.cloned.1.call-update) | async-done | bytes 1048592 | tf_op jit(solution)/shard_map/psum | solution.py:110
  535.0 2.3 divide_bitcast_fusion
  537.3 5.0 gather_fusion.2
  (98 shorter events, 45.0 us)
Async XLA Ops:
  69.8 2.2 copy-start.3
  72.4 3.8 copy-start
  72.4 32.6 %collective-permute-start = (bf16[1,512,1024]{2,1,0:T(8,128)(2,1)S(1)}, bf16[1,512,1024]{2,1,0:T(8,128)(2,1)}, u32[]{:S(2)}, u32[]{:S(2)}) collective-permute-start(bf16[1,512,1024]{2,1,0:T(8,128)(2,1)S(1)} %get-tuple-element.52), channel_id=1, source_target_pairs={{0,8},{8,0},{16,24},{24,16},{1,9},{9,1},{17,25},{25,17},{2,10},{10... | collective-permute-start | bytes 3145736 | tf_op jit(solution)/shard_map/ppermute | solution.py:22
  75.1 32.3 %collective-permute-start.1 = (bf16[1,512,1024]{2,1,0:T(8,128)(2,1)S(1)}, bf16[1,512,1024]{2,1,0:T(8,128)(2,1)}, u32[]{:S(2)}, u32[]{:S(2)}) collective-permute-start(bf16[1,512,1024]{2,1,0:T(8,128)(2,1)S(1)} %get-tuple-element.51), channel_id=1, source_target_pairs={{0,16},{8,24},{16,0},{24,8},{1,17},{9,25},{17,1},{25,9},{2,18},{10... | collective-permute-start | bytes 3145736 | tf_op jit(solution)/shard_map/ppermute | solution.py:22
  76.2 28.6 %copy-start.11 = (s32[1,256]{1,0:T(1,128)S(1)}, s32[1,256]{1,0:T(1,128)}, u32[]{:S(2)}) copy-start(s32[1,256]{1,0:T(1,128)} %param.7) | copy-start | bytes 3076
  96.8 8.2 %all-to-all-start = ((s32[4,1,512]{2,1,0:T(1,128)}), s32[4,1,512]{2,1,0:T(1,128)S(1)}, u32[]{:S(2)}, u32[]{:S(2)}) async-start(s32[4,1,512]{2,1,0:T(1,128)} %bitcast.6), calls=%async_computation | async-start | bytes 16384 | tf_op jit(solution)/shard_map/all_to_all | solution.py:79
  100.1 206.9 %all-reduce.8.cloned.1.call-start = ((), (), s32[]{:S(2)}) async-start(), calls=%async_computation.2 | async-start | bytes 2097152 | tf_op jit(solution)/shard_map/psum | solution.py:106
  100.1 24.8 %collective-permute-start.2 = (bf16[1,512,1024]{2,1,0:T(8,128)(2,1)S(1)}, bf16[1,512,1024]{2,1,0:T(8,128)(2,1)}, u32[]{:S(2)}, u32[]{:S(2)}) collective-permute-start(bf16[1,512,1024]{2,1,0:T(8,128)(2,1)S(1)} %get-tuple-element.50), channel_id=1, source_target_pairs={{0,24},{8,16},{16,8},{24,0},{1,25},{9,17},{17,9},{25,1},{2,26},{10... | collective-permute-start | bytes 3145736 | tf_op jit(solution)/shard_map/ppermute | solution.py:22
  127.2 3.4 copy-start.1
  131.4 1.9 copy-start.9
  194.1 17.1 %copy-start.6 = (f32[2048,256]{1,0:T(8,128)}, f32[2048,256]{1,0:T(8,128)S(1)}, u32[]{:S(2)}) copy-start(f32[2048,256]{1,0:T(8,128)S(1)} %get-tuple-element.57) | copy-start | bytes 6291460
  228.9 15.8 %copy-start.7 = (f32[2048,256]{1,0:T(8,128)S(1)}, f32[2048,256]{1,0:T(8,128)}, u32[]{:S(2)}) copy-start(f32[2048,256]{1,0:T(8,128)} %get-tuple-element.47) | copy-start | bytes 6291460
  249.7 171.6 %all-reduce.10.cloned.1.call-start = ((), (), s32[]{:S(2)}) async-start(), calls=%async_computation.3 | async-start | bytes 2097152 | tf_op jit(solution)/shard_map/psum | solution.py:106
  311.9 14.0 %copy-start.4 = (f32[2048,256]{1,0:T(8,128)}, f32[2048,256]{1,0:T(8,128)S(1)}, u32[]{:S(2)}) copy-start(f32[2048,256]{1,0:T(8,128)S(1)} %get-tuple-element.59) | copy-start | bytes 6291460
  343.6 15.7 %copy-start.8 = (f32[2048,256]{1,0:T(8,128)S(1)}, f32[2048,256]{1,0:T(8,128)}, u32[]{:S(2)}) copy-start(f32[2048,256]{1,0:T(8,128)} %get-tuple-element.43) | copy-start | bytes 6291460
  364.2 170.8 %all-reduce.12.cloned.1.call-start = ((), (), s32[]{:S(2)}) async-start(), calls=%async_computation.4 | async-start | bytes 2097152 | tf_op jit(solution)/shard_map/psum | solution.py:110
  426.3 14.0 %copy-start.5 = (f32[2048,256]{1,0:T(8,128)}, f32[2048,256]{1,0:T(8,128)S(1)}, u32[]{:S(2)}) copy-start(f32[2048,256]{1,0:T(8,128)S(1)} %get-tuple-element.61) | copy-start | bytes 6291460
  442.3 14.0 %copy-start.2 = (f32[2048,256]{1,0:T(8,128)}, f32[2048,256]{1,0:T(8,128)S(1)}, u32[]{:S(2)}) copy-start(f32[2048,256]{1,0:T(8,128)S(1)} %get-tuple-element.41) | copy-start | bytes 6291460
  471.8 2.6 copy-start.10
  477.9 59.5 %all-to-all-start.1 = ((bf16[4,512,256]{2,1,0:T(8,128)(2,1)}), bf16[4,512,256]{2,1,0:T(8,128)(2,1)S(1)}, u32[]{:S(2)}, u32[]{:S(2)}) async-start(bf16[4,512,256]{2,1,0:T(8,128)(2,1)} %bitcast.11), calls=%async_computation.1 | async-start | bytes 2097152 | tf_op jit(solution)/shard_map/all_to_all | solution.py:113
Sparse Core Ops, SparseCore 0:
  249.8 57.0 all-reduce.7
  364.3 56.9 all-reduce.9
  478.0 56.9 all-reduce.11
